TPU v7x, 512 devices: a whole 4x8x8 slice. The times are simulated.
512 devices in a mesh: tm: 64 (over z_hi, x, y), space: 8 (over z_lo, core).
Axes of the slice: x: 4, y: 8, z: 8 (z_hi: 2, z_lo: 4; z = z_hi * 4 + z_lo), core: 2. Of those that a mesh axis runs over, the one named last changes fastest.
Arguments:
- start_states: float32 [64, 128, 16, 128], P('tm', 'space'), may hold values from -6 to 6
- material: int32 [128, 16, 128], P('space'), may hold values from 0 to 15
- source: float32 [128, 16, 128], P('space'), may hold values from -0.6 to 0.6
- conductivity: float32 [16], replicated, may hold values from 0.02 to 0.16
- tide_amp: float32 [12], replicated, may hold values from -1.5 to 1.5
- phase: int32 [64], P('tm'), may hold values from 0 to 11
- coarse_rate: float32 [32, 4, 32], P('space'), may hold values from 0.3 to 40
Outputs:
- final_states: float32 [64, 128, 16, 128], P('tm', 'space')
All inputs are finite; a program needn't handle non-finite values.
Results may differ from a plain program's by a relative error of at most 0.00013.
Values sent between devices are 32-bit elements; how exact they have to be, the bound alone decides.
A program may use at most 64 MiB of HBM per device.

v0:
```python
import jax
import jax.numpy as jnp
from jax import lax
from jax.sharding import PartitionSpec as P

FINE = 10
ITERS = 2


def padded_2(block, sides, width):
    for axis, dim in sides:
        count = lax.axis_size(axis)
        forward = [(i, i + 1) for i in range(count - 1)]
        backward = [(target, source) for source, target in forward]
        low = lax.ppermute(
            lax.slice_in_dim(block, block.shape[dim] - width, None, axis=dim), axis, forward
        )
        high = lax.ppermute(lax.slice_in_dim(block, 0, width, axis=dim), axis, backward)
        block = jnp.concatenate([low, block, high], axis=dim)
    return block


def from_behind(block, axis, distance):
    devices = range(lax.axis_size(axis))
    route = [((i - distance) % len(devices), i) for i in devices]
    return lax.ppermute(block, axis, route)


def lookup_coef(material, conductivity):
    result = jnp.zeros(material.shape, jnp.float32)
    for class_id in range(conductivity.shape[0]):
        result = jnp.where(material == class_id, conductivity[class_id], result)
    return result


def neighbour_total(padded):
    framed = jnp.pad(padded, ((0, 0), (1, 1), (1, 1)))
    total = framed[2:, 1:-1, 1:-1] + framed[:-2, 1:-1, 1:-1]
    total = total + framed[1:-1, 2:, 1:-1] + framed[1:-1, :-2, 1:-1]
    total = total + framed[1:-1, 1:-1, 2:] + framed[1:-1, 1:-1, :-2]
    return total


def slab_update(field_now, cell_coef, forcing):
    padded = padded_2(field_now, (("space", 0),), 1)
    neighbours = neighbour_total(padded)
    return field_now + cell_coef * (neighbours - 6.0 * field_now) + forcing


def restrict(field_now):
    depth, rows, cols = field_now.shape
    blocks = field_now.reshape((depth // 4, 4, rows // 4, 4, cols // 4, 4))
    return blocks.mean(axis=(1, 3, 5))


def prolong(coarse):
    depth, rows, cols = coarse.shape
    wide = jnp.broadcast_to(coarse[:, None, :, None, :, None], (depth, 4, rows, 4, cols, 4))
    return wide.reshape((depth * 4, rows * 4, cols * 4))


def body(start_states, material, source, conductivity, tide_amp, phase, coarse_rate):
    windows = lax.axis_size("tm")
    device_index = lax.axis_index("tm")
    cell_coef = lookup_coef(material, conductivity)
    phase_ids = jnp.arange(tide_amp.shape[0], dtype=jnp.int32)
    decay = jnp.exp(-coarse_rate / windows)
    closure = 1.0 - jnp.exp(-coarse_rate)
    field_now = start_states[0]
    for outer in range(ITERS):
        tide_level = jnp.sum(jnp.where(phase_ids == phase[0], tide_amp, 0.0))
        forcing = tide_level * source
        finish = field_now
        for substep in range(FINE):
            finish = slab_update(finish, cell_coef, forcing)
        coarse_start = restrict(field_now)
        jump_now = restrict(finish) - decay * coarse_start
        pieces = lax.all_gather(jump_now[None], "tm", axis=0, tiled=True)
        count = pieces.shape[0]
        seen = jnp.arange(count, dtype=jnp.int32)
        lagged = (device_index - 1 - seen) % windows
        weights = jnp.exp(
            -coarse_rate[None] * lagged.astype(jnp.float32)[:, None, None, None] / windows
        )
        gathered_sum = jnp.sum(weights * pieces, axis=0)
        coarse = gathered_sum / closure
        corrected = finish + prolong(decay * (coarse - coarse_start))
        field_now = from_behind(corrected, "tm", 1)
    return field_now[None]


def solution(mesh):
    placed = (
        P("tm", "space", None, None),
        P("space", None, None),
        P("space", None, None),
        P(),
        P(),
        P("tm"),
        P("space", None, None),
    )
    return jax.shard_map(
        body, mesh=mesh, in_specs=placed, out_specs=P("tm", "space", None, None), check_vma=False
    )
```

profile of v0, /device:TPU:64, one launch (start us, length us, event | category | flops | bytes accessed | tf_op | source)
XLA Modules:
  0.0 887.4 jit_solution(9521776563705246436)
XLA Ops:
  2.7 3.6 collective-permute-start
  7.0 2.0 fusion.126
  11.3 11.9 %fusion.101 = f32[16,16,128]{2,1,0:T(8,128)S(1)} fusion(f32[16,16,128]{2,1,0:T(8,128)} %bitcast.35, f32[18,18,130]{2,1,0:T(8,128)S(1)} %select_maximum_fusion.38, f32[1,16,128]{2,1,0:T(8,128)S(1)} %collective-permute-done.1, f32[1,16,128]{2,1,0:T(8,128)S(1)} %collective-permute-done, f32[16,16,128]{2,1,0:T(8,128)} %param.9, f32[]{:T(128)} %fusion.103, ...), kind=kLoop, calls=%fused_computation.263 | loop fusion | flops 1474560 | bytes 1065028 | tf_op jit(solution)/shard_map/add | solution.py:47
  23.3 2.7 collective-permute-start.3
  25.9 3.9 collective-permute-start.2
  31.4 11.8 %fusion.96 = f32[16,16,128]{2,1,0:T(8,128)S(1)} fusion(f32[16,16,128]{2,1,0:T(8,128)S(1)} %fusion.101, f32[18,18,130]{2,1,0:T(8,128)S(1)} %select_maximum_fusion.36, f32[1,16,128]{2,1,0:T(8,128)S(1)} %collective-permute-done.3, f32[1,16,128]{2,1,0:T(8,128)S(1)} %collective-permute-done.2, f32[16,16,128]{2,1,0:T(8,128)} %param.9, f32[]{:T(128)} %fusion.103, ...), kind=kLoop, calls=%fused_computation.252 | loop fusion | flops 1474560 | bytes 1065028 | tf_op jit(solution)/shard_map/add | solution.py:47
  43.2 3.3 collective-permute-start.5
  46.5 2.2 collective-permute-start.4
  50.3 10.8 %fusion.91 = f32[16,16,128]{2,1,0:T(8,128)S(1)} fusion(f32[16,16,128]{2,1,0:T(8,128)S(1)} %fusion.96, f32[18,18,130]{2,1,0:T(8,128)S(1)} %select_maximum_fusion.34, f32[1,16,128]{2,1,0:T(8,128)S(1)} %collective-permute-done.5, f32[1,16,128]{2,1,0:T(8,128)S(1)} %collective-permute-done.4, f32[16,16,128]{2,1,0:T(8,128)S(1)} %copy-done, f32[]{:T(128)} %fusion.103, ...), kind=kLoop, calls=%fused_computation.241 | loop fusion | flops 1474560 | bytes 1065028 | tf_op jit(solution)/shard_map/add | solution.py:47
  61.1 4.1 collective-permute-start.7
  68.6 10.8 %fusion.86 = f32[16,16,128]{2,1,0:T(8,128)S(1)} fusion(f32[16,16,128]{2,1,0:T(8,128)S(1)} %fusion.91, f32[18,18,130]{2,1,0:T(8,128)S(1)} %select_maximum_fusion.32, f32[1,16,128]{2,1,0:T(8,128)S(1)} %collective-permute-done.7, f32[1,16,128]{2,1,0:T(8,128)S(1)} %collective-permute-done.6, f32[16,16,128]{2,1,0:T(8,128)S(1)} %copy-done, f32[]{:T(128)} %fusion.103, ...), kind=kLoop, calls=%fused_computation.230 | loop fusion | flops 1474560 | bytes 1065028 | tf_op jit(solution)/shard_map/add | solution.py:47
  79.5 3.6 collective-permute-start.9
  83.1 2.1 collective-permute-start.8
  86.7 10.8 %fusion.81 = f32[16,16,128]{2,1,0:T(8,128)S(1)} fusion(f32[16,16,128]{2,1,0:T(8,128)S(1)} %fusion.86, f32[18,18,130]{2,1,0:T(8,128)S(1)} %select_maximum_fusion.30, f32[1,16,128]{2,1,0:T(8,128)S(1)} %collective-permute-done.9, f32[1,16,128]{2,1,0:T(8,128)S(1)} %collective-permute-done.8, f32[16,16,128]{2,1,0:T(8,128)S(1)} %copy-done, f32[]{:T(128)} %fusion.103, ...), kind=kLoop, calls=%fused_computation.219 | loop fusion | flops 1474560 | bytes 1065028 | tf_op jit(solution)/shard_map/add | solution.py:47
  97.5 3.6 collective-permute-start.11
  104.6 10.8 %fusion.76 = f32[16,16,128]{2,1,0:T(8,128)S(1)} fusion(f32[16,16,128]{2,1,0:T(8,128)S(1)} %fusion.81, f32[18,18,130]{2,1,0:T(8,128)S(1)} %select_maximum_fusion.28, f32[1,16,128]{2,1,0:T(8,128)S(1)} %collective-permute-done.11, f32[1,16,128]{2,1,0:T(8,128)S(1)} %collective-permute-done.10, f32[16,16,128]{2,1,0:T(8,128)S(1)} %copy-done, f32[]{:T(128)} %fusion.103, ...), kind=kLoop, calls=%fused_computation.208 | loop fusion | flops 1474560 | bytes 1065028 | tf_op jit(solution)/shard_map/add | solution.py:47
  115.5 3.6 collective-permute-start.13
  122.6 10.8 %fusion.71 = f32[16,16,128]{2,1,0:T(8,128)S(1)} fusion(f32[16,16,128]{2,1,0:T(8,128)S(1)} %fusion.76, f32[18,18,130]{2,1,0:T(8,128)S(1)} %select_maximum_fusion.26, f32[1,16,128]{2,1,0:T(8,128)S(1)} %collective-permute-done.13, f32[1,16,128]{2,1,0:T(8,128)S(1)} %collective-permute-done.12, f32[16,16,128]{2,1,0:T(8,128)S(1)} %copy-done, f32[]{:T(128)} %fusion.103, ...), kind=kLoop, calls=%fused_computation.197 | loop fusion | flops 1474560 | bytes 1065028 | tf_op jit(solution)/shard_map/add | solution.py:47
  133.4 3.6 collective-permute-start.15
  137.0 1.9 collective-permute-start.14
  140.5 10.8 %fusion.66 = f32[16,16,128]{2,1,0:T(8,128)S(1)} fusion(f32[16,16,128]{2,1,0:T(8,128)S(1)} %fusion.71, f32[18,18,130]{2,1,0:T(8,128)S(1)} %select_maximum_fusion.24, f32[1,16,128]{2,1,0:T(8,128)S(1)} %collective-permute-done.15, f32[1,16,128]{2,1,0:T(8,128)S(1)} %collective-permute-done.14, f32[16,16,128]{2,1,0:T(8,128)S(1)} %copy-done, f32[]{:T(128)} %fusion.103, ...), kind=kLoop, calls=%fused_computation.186 | loop fusion | flops 1474560 | bytes 1065028 | tf_op jit(solution)/shard_map/add | solution.py:47
  151.3 3.6 collective-permute-start.17
  155.0 1.9 collective-permute-start.16
  158.4 10.8 %fusion.61 = f32[16,16,128]{2,1,0:T(8,128)S(1)} fusion(f32[16,16,128]{2,1,0:T(8,128)S(1)} %fusion.66, f32[18,18,130]{2,1,0:T(8,128)S(1)} %select_maximum_fusion.22, f32[1,16,128]{2,1,0:T(8,128)S(1)} %collective-permute-done.17, f32[1,16,128]{2,1,0:T(8,128)S(1)} %collective-permute-done.16, f32[16,16,128]{2,1,0:T(8,128)S(1)} %copy-done, f32[]{:T(128)} %fusion.103, ...), kind=kLoop, calls=%fused_computation.175 | loop fusion | flops 1474560 | bytes 1065028 | tf_op jit(solution)/shard_map/add | solution.py:47
  169.2 3.6 collective-permute-start.19
  174.8 5.7 reshape_squeeze.3
  180.5 2.6 reduce_sum.69
  183.3 10.8 %fusion.56 = f32[16,16,128]{2,1,0:T(8,128)S(1)} fusion(f32[16,16,128]{2,1,0:T(8,128)S(1)} %fusion.61, f32[18,18,130]{2,1,0:T(8,128)S(1)} %select_maximum_fusion.20, f32[1,16,128]{2,1,0:T(8,128)S(1)} %collective-permute-done.19, f32[1,16,128]{2,1,0:T(8,128)S(1)} %collective-permute-done.18, f32[16,16,128]{2,1,0:T(8,128)S(1)} %copy-done, f32[]{:T(128)} %fusion.103, ...), kind=kLoop, calls=%fused_computation.164 | loop fusion | flops 1474560 | bytes 1065028 | tf_op jit(solution)/shard_map/add | solution.py:47
  194.2 5.7 reshape.37
  199.8 2.6 reduce_sum.68
  202.5 227.3 %all-gather = f32[256,4,32]{2,1,0:T(4,128)S(1)} all-gather(f32[4,4,32]{2,1,0:T(4,128)S(1)} %get-tuple-element.46), channel_id=2, replica_groups=mesh['tm'=64,'space'=8] {'tm'}, dimensions={0}, use_global_device_ids=true | all-gather | bytes 133120 | tf_op jit(solution)/shard_map/all_gather | solution.py:78
  430.1 2.6 broadcast_in_dim.101
  432.7 4.9 reshape.38
  439.5 13.1 %collective-permute-done.20 = f32[16,16,128]{2,1,0:T(8,128)S(1)} collective-permute-done((f32[16,16,128]{2,1,0:T(8,128)S(1)}, f32[16,16,128]{2,1,0:T(8,128)S(1)}, u32[]{:S(2)}, u32[]{:S(2)}) %collective-permute-start.20) | collective-permute-done | bytes 131104 | tf_op jit(solution)/shard_map/ppermute | solution.py:26
  454.5 3.6 collective-permute-start.21
  459.7 10.8 %fusion.51 = f32[16,16,128]{2,1,0:T(8,128)S(1)} fusion(f32[16,16,128]{2,1,0:T(8,128)S(1)} %collective-permute-done.20, f32[18,18,130]{2,1,0:T(8,128)S(1)} %select_maximum_fusion.18, f32[1,16,128]{2,1,0:T(8,128)S(1)} %collective-permute-done.22, f32[1,16,128]{2,1,0:T(8,128)S(1)} %collective-permute-done.21, f32[16,16,128]{2,1,0:T(8,128)S(1)} %copy-done, ...), kind=kLoop, calls=%fused_computation.153 | loop fusion | flops 1474560 | bytes 1065028 | tf_op jit(solution)/shard_map/add | solution.py:47
  470.5 4.3 collective-permute-start.24
  478.2 10.8 %fusion.46 = f32[16,16,128]{2,1,0:T(8,128)S(1)} fusion(f32[16,16,128]{2,1,0:T(8,128)S(1)} %fusion.51, f32[18,18,130]{2,1,0:T(8,128)S(1)} %select_maximum_fusion.16, f32[1,16,128]{2,1,0:T(8,128)S(1)} %collective-permute-done.24, f32[1,16,128]{2,1,0:T(8,128)S(1)} %collective-permute-done.23, f32[16,16,128]{2,1,0:T(8,128)S(1)} %copy-done, f32[]{:T(128)} %fusion.103, ...), kind=kLoop, calls=%fused_computation.142 | loop fusion | flops 1474560 | bytes 1065028 | tf_op jit(solution)/shard_map/add | solution.py:47
  489.1 3.6 collective-permute-start.26
  496.2 10.8 %fusion.41 = f32[16,16,128]{2,1,0:T(8,128)S(1)} fusion(f32[16,16,128]{2,1,0:T(8,128)S(1)} %fusion.46, f32[18,18,130]{2,1,0:T(8,128)S(1)} %select_maximum_fusion.14, f32[1,16,128]{2,1,0:T(8,128)S(1)} %collective-permute-done.26, f32[1,16,128]{2,1,0:T(8,128)S(1)} %collective-permute-done.25, f32[16,16,128]{2,1,0:T(8,128)S(1)} %copy-done, f32[]{:T(128)} %fusion.103, ...), kind=kLoop, calls=%fused_computation.131 | loop fusion | flops 1474560 | bytes 1065028 | tf_op jit(solution)/shard_map/add | solution.py:47
  507.0 3.6 collective-permute-start.28
  514.1 10.8 %fusion.36 = f32[16,16,128]{2,1,0:T(8,128)S(1)} fusion(f32[16,16,128]{2,1,0:T(8,128)S(1)} %fusion.41, f32[18,18,130]{2,1,0:T(8,128)S(1)} %select_maximum_fusion.12, f32[1,16,128]{2,1,0:T(8,128)S(1)} %collective-permute-done.28, f32[1,16,128]{2,1,0:T(8,128)S(1)} %collective-permute-done.27, f32[16,16,128]{2,1,0:T(8,128)S(1)} %copy-done, f32[]{:T(128)} %fusion.103, ...), kind=kLoop, calls=%fused_computation.120 | loop fusion | flops 1474560 | bytes 1065028 | tf_op jit(solution)/shard_map/add | solution.py:47
  524.9 3.6 collective-permute-start.30
  532.0 10.8 %fusion.31 = f32[16,16,128]{2,1,0:T(8,128)S(1)} fusion(f32[16,16,128]{2,1,0:T(8,128)S(1)} %fusion.36, f32[18,18,130]{2,1,0:T(8,128)S(1)} %select_maximum_fusion.10, f32[1,16,128]{2,1,0:T(8,128)S(1)} %collective-permute-done.30, f32[1,16,128]{2,1,0:T(8,128)S(1)} %collective-permute-done.29, f32[16,16,128]{2,1,0:T(8,128)S(1)} %copy-done, f32[]{:T(128)} %fusion.103, ...), kind=kLoop, calls=%fused_computation.109 | loop fusion | flops 1474560 | bytes 1065028 | tf_op jit(solution)/shard_map/add | solution.py:47
  542.8 3.6 collective-permute-start.32
  549.9 10.8 %fusion.26 = f32[16,16,128]{2,1,0:T(8,128)S(1)} fusion(f32[16,16,128]{2,1,0:T(8,128)S(1)} %fusion.31, f32[18,18,130]{2,1,0:T(8,128)S(1)} %select_maximum_fusion.8, f32[1,16,128]{2,1,0:T(8,128)S(1)} %collective-permute-done.32, f32[1,16,128]{2,1,0:T(8,128)S(1)} %collective-permute-done.31, f32[16,16,128]{2,1,0:T(8,128)S(1)} %copy-done, f32[]{:T(128)} %fusion.103, ...), kind=kLoop, calls=%fused_computation.98 | loop fusion | flops 1474560 | bytes 1065028 | tf_op jit(solution)/shard_map/add | solution.py:47
  560.8 3.6 collective-permute-start.34
  567.9 10.8 %fusion.21 = f32[16,16,128]{2,1,0:T(8,128)S(1)} fusion(f32[16,16,128]{2,1,0:T(8,128)S(1)} %fusion.26, f32[18,18,130]{2,1,0:T(8,128)S(1)} %select_maximum_fusion.6, f32[1,16,128]{2,1,0:T(8,128)S(1)} %collective-permute-done.34, f32[1,16,128]{2,1,0:T(8,128)S(1)} %collective-permute-done.33, f32[16,16,128]{2,1,0:T(8,128)S(1)} %copy-done, f32[]{:T(128)} %fusion.103, ...), kind=kLoop, calls=%fused_computation.87 | loop fusion | flops 1474560 | bytes 1065028 | tf_op jit(solution)/shard_map/add | solution.py:47
  578.7 3.6 collective-permute-start.36
  585.8 10.8 %fusion.16 = f32[16,16,128]{2,1,0:T(8,128)S(1)} fusion(f32[16,16,128]{2,1,0:T(8,128)S(1)} %fusion.21, f32[18,18,130]{2,1,0:T(8,128)S(1)} %select_maximum_fusion.4, f32[1,16,128]{2,1,0:T(8,128)S(1)} %collective-permute-done.36, f32[1,16,128]{2,1,0:T(8,128)S(1)} %collective-permute-done.35, f32[16,16,128]{2,1,0:T(8,128)S(1)} %copy-done, f32[]{:T(128)} %fusion.103, ...), kind=kLoop, calls=%fused_computation.76 | loop fusion | flops 1474560 | bytes 1065028 | tf_op jit(solution)/shard_map/add | solution.py:47
  596.6 3.6 collective-permute-start.38
  603.7 10.8 %fusion.11 = f32[16,16,128]{2,1,0:T(8,128)S(1)} fusion(f32[16,16,128]{2,1,0:T(8,128)S(1)} %fusion.16, f32[18,18,130]{2,1,0:T(8,128)S(1)} %select_maximum_fusion.2, f32[1,16,128]{2,1,0:T(8,128)S(1)} %collective-permute-done.38, f32[1,16,128]{2,1,0:T(8,128)S(1)} %collective-permute-done.37, f32[16,16,128]{2,1,0:T(8,128)S(1)} %copy-done, f32[]{:T(128)} %fusion.103, ...), kind=kLoop, calls=%fused_computation.65 | loop fusion | flops 1474560 | bytes 1065028 | tf_op jit(solution)/shard_map/add | solution.py:47
  614.5 3.6 collective-permute-start.40
  618.2 2.1 collective-permute-start.39
  620.3 5.7 reshape.40
  626.0 2.6 reduce_sum.72
  628.8 10.8 %fusion.6 = f32[16,16,128]{2,1,0:T(8,128)S(1)} fusion(f32[16,16,128]{2,1,0:T(8,128)S(1)} %fusion.11, f32[18,18,130]{2,1,0:T(8,128)S(1)} %select_maximum_fusion, f32[1,16,128]{2,1,0:T(8,128)S(1)} %collective-permute-done.40, f32[1,16,128]{2,1,0:T(8,128)S(1)} %collective-permute-done.39, f32[16,16,128]{2,1,0:T(8,128)S(1)} %copy-done, f32[]{:T(128)} %fusion.103, ...), kind=kLoop, calls=%fused_computation.54 | loop fusion | flops 1474560 | bytes 1065028 | tf_op jit(solution)/shard_map/add | solution.py:47
  639.6 5.7 reshape.39
  645.3 2.6 reduce_sum.71
  647.9 215.9 %all-gather.1 = f32[256,4,32]{2,1,0:T(4,128)S(1)} all-gather(f32[4,4,32]{2,1,0:T(4,128)S(1)} %multiply_subtract_fusion), channel_id=3, replica_groups=mesh['tm'=64,'space'=8] {'tm'}, dimensions={0}, use_global_device_ids=true | all-gather | bytes 133120 | tf_op jit(solution)/shard_map/all_gather | solution.py:78
  864.3 2.6 broadcast_in_dim.103
  866.8 4.9 reshape.41
  871.7 3.2 collective-permute-start.41
  874.9 11.8 %collective-permute-done.41 = f32[16,16,128]{2,1,0:T(8,128)S(1)} collective-permute-done((f32[16,16,128]{2,1,0:T(8,128)S(1)}, f32[16,16,128]{2,1,0:T(8,128)S(1)}, u32[]{:S(2)}, u32[]{:S(2)}) %collective-permute-start.41) | collective-permute-done | bytes 131104 | tf_op jit(solution)/shard_map/ppermute | solution.py:26
  (114 shorter events, 59.6 us)
Async XLA Ops:
  0.0 50.3 %copy-start = (f32[16,16,128]{2,1,0:T(8,128)S(1)}, f32[16,16,128]{2,1,0:T(8,128)}, u32[]{:S(2)}) copy-start(f32[16,16,128]{2,1,0:T(8,128)} %param.9) | copy-start | bytes 393220
  0.0 50.3 %copy-start.1 = (s32[16,16,128]{2,1,0:T(8,128)S(1)}, s32[16,16,128]{2,1,0:T(8,128)}, u32[]{:S(2)}) copy-start(s32[16,16,128]{2,1,0:T(8,128)} %param.8) | copy-start | bytes 393220
  0.8 9.4 %collective-permute-start.1 = (f32[1,16,128]{2,1,0:T(8,128)S(1)}, f32[1,16,128]{2,1,0:T(8,128)S(1)}, u32[]{:S(2)}, u32[]{:S(2)}) collective-permute-start(f32[1,16,128]{2,1,0:T(8,128)S(1)} %get-tuple-element.43), channel_id=1, source_target_pairs={{0,1},{1,2},{2,3},{3,4},{4,5},{5,6},{6,7},{8,9},{9,10},{10,11},{11... | collective-permute-start | bytes 24584 | tf_op jit(solution)/shard_map/ppermute | solution.py:15
  2.7 7.5 collective-permute-start
  23.3 6.6 collective-permute-start.3
  25.9 5.3 collective-permute-start.2
  43.2 5.6 collective-permute-start.5
  46.5 3.6 collective-permute-start.4
  61.1 6.0 collective-permute-start.7
  65.2 3.3 collective-permute-start.6
  79.5 5.7 collective-permute-start.9
  83.1 91.7 %copy-start.2 = (f32[1,16,16,128]{3,2,1,0:T(8,128)S(1)}, f32[1,16,16,128]{3,2,1,0:T(8,128)}, u32[]{:S(2)}) copy-start(f32[1,16,16,128]{3,2,1,0:T(8,128)} %param.7) | copy-start | bytes 393220
  83.1 3.4 collective-permute-start.8
  97.5 5.6 collective-permute-start.11
  101.2 3.3 collective-permute-start.10
  115.5 5.6 collective-permute-start.13
  119.1 3.3 collective-permute-start.12
  133.4 5.6 collective-permute-start.15
  137.0 3.3 collective-permute-start.14
  151.3 5.6 collective-permute-start.17
  155.0 3.3 collective-permute-start.16
  169.2 13.9 %collective-permute-start.19 = (f32[1,16,128]{2,1,0:T(8,128)S(1)}, f32[1,16,128]{2,1,0:T(8,128)S(1)}, u32[]{:S(2)}, u32[]{:S(2)}) collective-permute-start(f32[1,16,128]{2,1,0:T(8,128)S(1)} %get-tuple-element.25), channel_id=1, source_target_pairs={{0,1},{1,2},{2,3},{3,4},{4,5},{5,6},{6,7},{8,9},{9,10},{10,11},{11... | collective-permute-start | bytes 24584 | tf_op jit(solution)/shard_map/ppermute | solution.py:15
  172.9 10.3 %collective-permute-start.18 = (f32[1,16,128]{2,1,0:T(8,128)S(1)}, f32[1,16,128]{2,1,0:T(8,128)S(1)}, u32[]{:S(2)}, u32[]{:S(2)}) collective-permute-start(f32[1,16,128]{2,1,0:T(8,128)S(1)} %get-tuple-element.26), channel_id=1, source_target_pairs={{1,0},{2,1},{3,2},{4,3},{5,4},{6,5},{7,6},{9,8},{10,9},{11,10},{12... | collective-permute-start | bytes 24584 | tf_op jit(solution)/shard_map/ppermute | solution.py:18
  194.1 8.3 copy-start.3
  437.6 15.0 %collective-permute-start.20 = (f32[16,16,128]{2,1,0:T(8,128)S(1)}, f32[16,16,128]{2,1,0:T(8,128)S(1)}, u32[]{:S(2)}, u32[]{:S(2)}) collective-permute-start(f32[16,16,128]{2,1,0:T(8,128)S(1)} %add.550), channel_id=1, source_target_pairs={{504,0},{0,8},{8,16},{16,24},{24,32},{32,40},{40,48},{48,56},{56,6... | collective-permute-start | bytes 393224 | tf_op jit(solution)/shard_map/ppermute | solution.py:26
  452.6 5.6 collective-permute-start.22
  454.5 5.0 collective-permute-start.21
  470.5 6.2 collective-permute-start.24
  474.8 3.3 collective-permute-start.23
  489.1 5.6 collective-permute-start.26
  492.7 3.3 collective-permute-start.25
  507.0 5.6 collective-permute-start.28
  510.6 3.3 collective-permute-start.27
  524.9 5.6 collective-permute-start.30
  528.6 3.3 collective-permute-start.29
  542.8 5.6 collective-permute-start.32
  546.5 3.3 collective-permute-start.31
  560.8 5.6 collective-permute-start.34
  564.4 3.3 collective-permute-start.33
  578.7 5.6 collective-permute-start.36
  582.3 3.3 collective-permute-start.35
  596.6 5.6 collective-permute-start.38
  600.2 3.3 collective-permute-start.37
  614.5 14.1 %collective-permute-start.40 = (f32[1,16,128]{2,1,0:T(8,128)S(1)}, f32[1,16,128]{2,1,0:T(8,128)S(1)}, u32[]{:S(2)}, u32[]{:S(2)}) collective-permute-start(f32[1,16,128]{2,1,0:T(8,128)S(1)} %get-tuple-element.5), channel_id=1, source_target_pairs={{0,1},{1,2},{2,3},{3,4},{4,5},{5,6},{6,7},{8,9},{9,10},{10,11},{11... | collective-permute-start | bytes 24584 | tf_op jit(solution)/shard_map/ppermute | solution.py:15
  618.2 10.5 %collective-permute-start.39 = (f32[1,16,128]{2,1,0:T(8,128)S(1)}, f32[1,16,128]{2,1,0:T(8,128)S(1)}, u32[]{:S(2)}, u32[]{:S(2)}) collective-permute-start(f32[1,16,128]{2,1,0:T(8,128)S(1)} %get-tuple-element.6), channel_id=1, source_target_pairs={{1,0},{2,1},{3,2},{4,3},{5,4},{6,5},{7,6},{9,8},{10,9},{11,10},{12... | collective-permute-start | bytes 24584 | tf_op jit(solution)/shard_map/ppermute | solution.py:18
  871.7 15.0 %collective-permute-start.41 = (f32[16,16,128]{2,1,0:T(8,128)S(1)}, f32[16,16,128]{2,1,0:T(8,128)S(1)}, u32[]{:S(2)}, u32[]{:S(2)}) collective-permute-start(f32[16,16,128]{2,1,0:T(8,128)S(1)} %add.621), channel_id=1, source_target_pairs={{504,0},{0,8},{8,16},{16,24},{24,32},{32,40},{40,48},{48,56},{56,6... | collective-permute-start | bytes 393224 | tf_op jit(solution)/shard_map/ppermute | solution.py:26
where the time goes:
time: 892 us; the launch traced here: 887 us
  blocking collectives  443 us (50%)
  other arithmetic  235 us (26%)
  starting transfers between devices  119 us (13%)
  waiting for transfers between devices  47.6 us (5%)
  local copies, waits for them, and re-layouts  41.1 us (5%)
    all_gather x2, blocking collectives, body(): pieces = lax.all_gather(jump_now[None], 'tm', axis=0, tiled=True)  443 us
    add x20, other arithmetic, slab_update(): return field_now + cell_coef * (neighbours - 6.0 * field_now) + forcing  218 us
    ppermute x20, starting transfers between devices, padded_2(): lax.ppermute(lax.slice_in_dim(block, block.shape[dim] - width, None, axis...  69.2 us
    ppermute x20, starting transfers between devices, padded_2(): lax.ppermute(lax.slice_in_dim(block, 0, width, axis=dim), axis, backward)  44.5 us
    ppermute x2, waiting for transfers between devices, from_behind(): return lax.ppermute(block, axis, route)  24.9 us
    ppermute x20, waiting for transfers between devices, padded_2(): lax.ppermute(lax.slice_in_dim(block, 0, width, axis=dim), axis, backward)  22.7 us
  transfers between devices with their start and end apart: 42, of which 19 were waited for; matrix products, arithmetic and copies ran while one was open for 2% of the time, Pallas kernels for 0%

commit v1 on v0

--- a/solution.py
+++ b/solution.py
@@ -75,7 +75,9 @@
             finish = slab_update(finish, cell_coef, forcing)
         coarse_start = restrict(field_now)
         jump_now = restrict(finish) - decay * coarse_start
-        pieces = lax.all_gather(jump_now[None], "tm", axis=0, tiled=True)
+        pieces = jnp.concatenate(
+            lax.all_to_all(jnp.stack([jump_now[None]] * lax.axis_size("tm")), "tm", 0, 0), axis=0
+        )
         count = pieces.shape[0]
         seen = jnp.arange(count, dtype=jnp.int32)
         lagged = (device_index - 1 - seen) % windows

time: 892 us -> 508 us (0.57)
  the two profiles are of different devices: /device:TPU:64 before, /device:TPU:1 now
where the time goes in v1:
time: 508 us; the launch traced here: 503 us
  other arithmetic  236 us (46%)
  starting transfers between devices  116 us (23%)
  waiting for transfers between devices  86.2 us (17%)
  local copies, waits for them, and re-layouts  43.5 us (9%)
  blocking collectives  18.8 us (4%)
    add x20, other arithmetic, slab_update(): return field_now + cell_coef * (neighbours - 6.0 * field_now) + forcing  217 us
    ppermute x20, starting transfers between devices, padded_2(): lax.ppermute(lax.slice_in_dim(block, 0, width, axis=dim), axis, backward)  49.5 us
    ppermute x20, waiting for transfers between devices, padded_2(): lax.ppermute(lax.slice_in_dim(block, 0, width, axis=dim), axis, backward)  45.5 us
    ppermute x20, starting transfers between devices, padded_2(): lax.ppermute(lax.slice_in_dim(block, block.shape[dim] - width, None, axis...  45 us
    ppermute x2, waiting for transfers between devices, from_behind(): return lax.ppermute(block, axis, route)  26 us
    all_to_all x1, blocking collectives, body(): lax.all_to_all(jnp.stack([jump_now[None]] * lax.axis_size('tm')), 'tm', 0...  18.8 us
    reshape x3, local copies, waits for them, and re-layouts, restrict(): blocks = field_now.reshape((depth // 4, 4, rows // 4, 4, cols // 4, 4))  17 us
    all_to_all x1, starting transfers between devices, body(): lax.all_to_all(jnp.stack([jump_now[None]] * lax.axis_size('tm')), 'tm', 0...  16.6 us
  transfers between devices with their start and end apart: 43, of which 20 were waited for; matrix products, arithmetic and copies ran while one was open for 4% of the time, Pallas kernels for 0%

profile of v1, /device:TPU:1, one launch (start us, length us, event | category | flops | bytes accessed | tf_op | source)
XLA Modules:
  0.0 503.0 jit_solution(428362355162330608)
XLA Ops:
  0.8 5.4 %collective-permute-start.1 = (f32[1,16,128]{2,1,0:T(8,128)S(1)}, f32[1,16,128]{2,1,0:T(8,128)S(1)}, u32[]{:S(2)}, u32[]{:S(2)}) collective-permute-start(f32[1,16,128]{2,1,0:T(8,128)S(1)} %get-tuple-element.43), channel_id=1, source_target_pairs={{0,1},{1,2},{2,3},{3,4},{4,5},{5,6},{6,7},{8,9},{9,10},{10,11},{11... | collective-permute-start | bytes 24584 | tf_op jit(solution)/shard_map/ppermute | solution.py:15
  6.1 4.7 collective-permute-start
  15.7 11.9 %fusion.103 = f32[16,16,128]{2,1,0:T(8,128)S(1)} fusion(f32[16,16,128]{2,1,0:T(8,128)} %bitcast.39, f32[18,18,130]{2,1,0:T(8,128)S(1)} %select_maximum_fusion.38, f32[1,16,128]{2,1,0:T(8,128)S(1)} %collective-permute-done.1, f32[1,16,128]{2,1,0:T(8,128)S(1)} %collective-permute-done, f32[16,16,128]{2,1,0:T(8,128)} %param.9, f32[]{:T(128)} %fusion.105, ...), kind=kLoop, calls=%fused_computation.265 | loop fusion | flops 1474560 | bytes 1065028 | tf_op jit(solution)/shard_map/add | solution.py:47
  29.6 2.4 collective-permute-start.2
  32.0 2.5 collective-permute-done.2
  34.8 11.7 %fusion.98 = f32[16,16,128]{2,1,0:T(8,128)S(1)} fusion(f32[16,16,128]{2,1,0:T(8,128)S(1)} %fusion.103, f32[18,18,130]{2,1,0:T(8,128)S(1)} %select_maximum_fusion.36, f32[1,16,128]{2,1,0:T(8,128)S(1)} %collective-permute-done.3, f32[1,16,128]{2,1,0:T(8,128)S(1)} %collective-permute-done.2, f32[16,16,128]{2,1,0:T(8,128)} %param.9, f32[]{:T(128)} %fusion.105, ...), kind=kLoop, calls=%fused_computation.254 | loop fusion | flops 1474560 | bytes 1065028 | tf_op jit(solution)/shard_map/add | solution.py:47
  48.5 2.4 collective-permute-start.4
  50.9 2.6 collective-permute-done.4
  53.6 10.8 %fusion.93 = f32[16,16,128]{2,1,0:T(8,128)S(1)} fusion(f32[16,16,128]{2,1,0:T(8,128)S(1)} %fusion.98, f32[18,18,130]{2,1,0:T(8,128)S(1)} %select_maximum_fusion.34, f32[1,16,128]{2,1,0:T(8,128)S(1)} %collective-permute-done.5, f32[1,16,128]{2,1,0:T(8,128)S(1)} %collective-permute-done.4, f32[16,16,128]{2,1,0:T(8,128)S(1)} %copy-done, f32[]{:T(128)} %fusion.105, ...), kind=kLoop, calls=%fused_computation.243 | loop fusion | flops 1474560 | bytes 1065028 | tf_op jit(solution)/shard_map/add | solution.py:47
  66.4 2.4 collective-permute-start.6
  68.8 3.0 collective-permute-done.6
  71.9 10.8 %fusion.88 = f32[16,16,128]{2,1,0:T(8,128)S(1)} fusion(f32[16,16,128]{2,1,0:T(8,128)S(1)} %fusion.93, f32[18,18,130]{2,1,0:T(8,128)S(1)} %select_maximum_fusion.32, f32[1,16,128]{2,1,0:T(8,128)S(1)} %collective-permute-done.7, f32[1,16,128]{2,1,0:T(8,128)S(1)} %collective-permute-done.6, f32[16,16,128]{2,1,0:T(8,128)S(1)} %copy-done, f32[]{:T(128)} %fusion.105, ...), kind=kLoop, calls=%fused_computation.232 | loop fusion | flops 1474560 | bytes 1065028 | tf_op jit(solution)/shard_map/add | solution.py:47
  84.7 2.5 collective-permute-start.8
  87.2 2.6 collective-permute-done.8
  90.0 10.8 %fusion.83 = f32[16,16,128]{2,1,0:T(8,128)S(1)} fusion(f32[16,16,128]{2,1,0:T(8,128)S(1)} %fusion.88, f32[18,18,130]{2,1,0:T(8,128)S(1)} %select_maximum_fusion.30, f32[1,16,128]{2,1,0:T(8,128)S(1)} %collective-permute-done.9, f32[1,16,128]{2,1,0:T(8,128)S(1)} %collective-permute-done.8, f32[16,16,128]{2,1,0:T(8,128)S(1)} %copy-done, f32[]{:T(128)} %fusion.105, ...), kind=kLoop, calls=%fused_computation.221 | loop fusion | flops 1474560 | bytes 1065028 | tf_op jit(solution)/shard_map/add | solution.py:47
  105.1 2.6 collective-permute-done.10
  107.9 10.8 %fusion.78 = f32[16,16,128]{2,1,0:T(8,128)S(1)} fusion(f32[16,16,128]{2,1,0:T(8,128)S(1)} %fusion.83, f32[18,18,130]{2,1,0:T(8,128)S(1)} %select_maximum_fusion.28, f32[1,16,128]{2,1,0:T(8,128)S(1)} %collective-permute-done.11, f32[1,16,128]{2,1,0:T(8,128)S(1)} %collective-permute-done.10, f32[16,16,128]{2,1,0:T(8,128)S(1)} %copy-done, f32[]{:T(128)} %fusion.105, ...), kind=kLoop, calls=%fused_computation.210 | loop fusion | flops 1474560 | bytes 1065028 | tf_op jit(solution)/shard_map/add | solution.py:47
  123.0 2.6 collective-permute-done.12
  125.8 10.8 %fusion.73 = f32[16,16,128]{2,1,0:T(8,128)S(1)} fusion(f32[16,16,128]{2,1,0:T(8,128)S(1)} %fusion.78, f32[18,18,130]{2,1,0:T(8,128)S(1)} %select_maximum_fusion.26, f32[1,16,128]{2,1,0:T(8,128)S(1)} %collective-permute-done.13, f32[1,16,128]{2,1,0:T(8,128)S(1)} %collective-permute-done.12, f32[16,16,128]{2,1,0:T(8,128)S(1)} %copy-done, f32[]{:T(128)} %fusion.105, ...), kind=kLoop, calls=%fused_computation.199 | loop fusion | flops 1474560 | bytes 1065028 | tf_op jit(solution)/shard_map/add | solution.py:47
  140.9 2.6 collective-permute-done.14
  143.6 10.8 %fusion.68 = f32[16,16,128]{2,1,0:T(8,128)S(1)} fusion(f32[16,16,128]{2,1,0:T(8,128)S(1)} %fusion.73, f32[18,18,130]{2,1,0:T(8,128)S(1)} %select_maximum_fusion.24, f32[1,16,128]{2,1,0:T(8,128)S(1)} %collective-permute-done.15, f32[1,16,128]{2,1,0:T(8,128)S(1)} %collective-permute-done.14, f32[16,16,128]{2,1,0:T(8,128)S(1)} %copy-done, f32[]{:T(128)} %fusion.105, ...), kind=kLoop, calls=%fused_computation.188 | loop fusion | flops 1474560 | bytes 1065028 | tf_op jit(solution)/shard_map/add | solution.py:47
  158.8 2.6 collective-permute-done.16
  161.5 10.8 %fusion.63 = f32[16,16,128]{2,1,0:T(8,128)S(1)} fusion(f32[16,16,128]{2,1,0:T(8,128)S(1)} %fusion.68, f32[18,18,130]{2,1,0:T(8,128)S(1)} %select_maximum_fusion.22, f32[1,16,128]{2,1,0:T(8,128)S(1)} %collective-permute-done.17, f32[1,16,128]{2,1,0:T(8,128)S(1)} %collective-permute-done.16, f32[16,16,128]{2,1,0:T(8,128)S(1)} %copy-done, f32[]{:T(128)} %fusion.105, ...), kind=kLoop, calls=%fused_computation.177 | loop fusion | flops 1474560 | bytes 1065028 | tf_op jit(solution)/shard_map/add | solution.py:47
  176.7 5.7 %reshape_squeeze.3 = f32[4,4,4,4,32,4]{5,4,3,2,1,0:T(8,128)} reshape(f32[1,16,16,128]{3,2,1,0:T(8,128)S(1)} %copy-done.2) | data formatting | bytes 262144 | tf_op jit(solution)/shard_map/reshape;squeeze | solution.py:52
  182.3 2.6 reduce_sum.69
  185.2 10.8 %fusion.58 = f32[16,16,128]{2,1,0:T(8,128)S(1)} fusion(f32[16,16,128]{2,1,0:T(8,128)S(1)} %fusion.63, f32[18,18,130]{2,1,0:T(8,128)S(1)} %select_maximum_fusion.20, f32[1,16,128]{2,1,0:T(8,128)S(1)} %collective-permute-done.19, f32[1,16,128]{2,1,0:T(8,128)S(1)} %collective-permute-done.18, f32[16,16,128]{2,1,0:T(8,128)S(1)} %copy-done, f32[]{:T(128)} %fusion.105, ...), kind=kLoop, calls=%fused_computation.166 | loop fusion | flops 1474560 | bytes 1065028 | tf_op jit(solution)/shard_map/add | solution.py:47
  195.9 5.7 %reshape.47 = f32[4,4,4,4,32,4]{5,4,3,2,1,0:T(8,128)} reshape(f32[16,16,128]{2,1,0:T(8,128)S(1)} %fusion.58) | data formatting | bytes 262144 | tf_op jit(solution)/shard_map/reshape | solution.py:52
  201.6 2.6 reduce_sum.68
  205.3 16.6 %all-to-all-start = ((f32[64,1,512]{2,1,0:T(1,128)}), f32[64,1,512]{2,1,0:T(1,128)S(1)}, u32[]{:S(2)}, u32[]{:S(2)}) async-start(f32[64,1,512]{2,1,0:T(1,128)} %reshape.54), calls=%async_computation | async-start | bytes 262144 | tf_op jit(solution)/shard_map/all_to_all | solution.py:79
  221.9 14.6 %all-to-all-done = f32[64,1,512]{2,1,0:T(1,128)S(1)} async-done(((f32[64,1,512]{2,1,0:T(1,128)}), f32[64,1,512]{2,1,0:T(1,128)S(1)}, u32[]{:S(2)}, u32[]{:S(2)}) %all-to-all-start) | async-done | bytes 131104 | tf_op jit(solution)/shard_map/all_to_all | solution.py:79
  238.7 2.6 broadcast_in_dim.94
  241.2 4.9 reshape.49
  246.1 2.9 collective-permute-start.20
  249.0 12.3 %collective-permute-done.20 = f32[16,16,128]{2,1,0:T(8,128)S(1)} collective-permute-done((f32[16,16,128]{2,1,0:T(8,128)S(1)}, f32[16,16,128]{2,1,0:T(8,128)S(1)}, u32[]{:S(2)}, u32[]{:S(2)}) %collective-permute-start.20) | collective-permute-done | bytes 131104 | tf_op jit(solution)/shard_map/ppermute | solution.py:26
  261.2 4.4 collective-permute-start.22
  267.6 3.0 collective-permute-done.21
  270.8 10.8 %fusion.53 = f32[16,16,128]{2,1,0:T(8,128)S(1)} fusion(f32[16,16,128]{2,1,0:T(8,128)S(1)} %collective-permute-done.20, f32[18,18,130]{2,1,0:T(8,128)S(1)} %select_maximum_fusion.18, f32[1,16,128]{2,1,0:T(8,128)S(1)} %collective-permute-done.22, f32[1,16,128]{2,1,0:T(8,128)S(1)} %collective-permute-done.21, f32[16,16,128]{2,1,0:T(8,128)S(1)} %copy-done, ...), kind=kLoop, calls=%fused_computation.155 | loop fusion | flops 1474560 | bytes 1065028 | tf_op jit(solution)/shard_map/add | solution.py:47
  285.9 3.5 collective-permute-done.23
  289.6 10.8 %fusion.48 = f32[16,16,128]{2,1,0:T(8,128)S(1)} fusion(f32[16,16,128]{2,1,0:T(8,128)S(1)} %fusion.53, f32[18,18,130]{2,1,0:T(8,128)S(1)} %select_maximum_fusion.16, f32[1,16,128]{2,1,0:T(8,128)S(1)} %collective-permute-done.24, f32[1,16,128]{2,1,0:T(8,128)S(1)} %collective-permute-done.23, f32[16,16,128]{2,1,0:T(8,128)S(1)} %copy-done, f32[]{:T(128)} %fusion.105, ...), kind=kLoop, calls=%fused_computation.144 | loop fusion | flops 1474560 | bytes 1065028 | tf_op jit(solution)/shard_map/add | solution.py:47
  304.7 2.6 collective-permute-done.25
  307.5 10.8 %fusion.43 = f32[16,16,128]{2,1,0:T(8,128)S(1)} fusion(f32[16,16,128]{2,1,0:T(8,128)S(1)} %fusion.48, f32[18,18,130]{2,1,0:T(8,128)S(1)} %select_maximum_fusion.14, f32[1,16,128]{2,1,0:T(8,128)S(1)} %collective-permute-done.26, f32[1,16,128]{2,1,0:T(8,128)S(1)} %collective-permute-done.25, f32[16,16,128]{2,1,0:T(8,128)S(1)} %copy-done, f32[]{:T(128)} %fusion.105, ...), kind=kLoop, calls=%fused_computation.133 | loop fusion | flops 1474560 | bytes 1065028 | tf_op jit(solution)/shard_map/add | solution.py:47
  322.6 2.6 collective-permute-done.27
  325.4 10.8 %fusion.38 = f32[16,16,128]{2,1,0:T(8,128)S(1)} fusion(f32[16,16,128]{2,1,0:T(8,128)S(1)} %fusion.43, f32[18,18,130]{2,1,0:T(8,128)S(1)} %select_maximum_fusion.12, f32[1,16,128]{2,1,0:T(8,128)S(1)} %collective-permute-done.28, f32[1,16,128]{2,1,0:T(8,128)S(1)} %collective-permute-done.27, f32[16,16,128]{2,1,0:T(8,128)S(1)} %copy-done, f32[]{:T(128)} %fusion.105, ...), kind=kLoop, calls=%fused_computation.122 | loop fusion | flops 1474560 | bytes 1065028 | tf_op jit(solution)/shard_map/add | solution.py:47
  340.5 2.6 collective-permute-done.29
  343.3 10.8 %fusion.33 = f32[16,16,128]{2,1,0:T(8,128)S(1)} fusion(f32[16,16,128]{2,1,0:T(8,128)S(1)} %fusion.38, f32[18,18,130]{2,1,0:T(8,128)S(1)} %select_maximum_fusion.10, f32[1,16,128]{2,1,0:T(8,128)S(1)} %collective-permute-done.30, f32[1,16,128]{2,1,0:T(8,128)S(1)} %collective-permute-done.29, f32[16,16,128]{2,1,0:T(8,128)S(1)} %copy-done, f32[]{:T(128)} %fusion.105, ...), kind=kLoop, calls=%fused_computation.111 | loop fusion | flops 1474560 | bytes 1065028 | tf_op jit(solution)/shard_map/add | solution.py:47
  358.4 2.6 collective-permute-done.31
  361.1 10.8 %fusion.28 = f32[16,16,128]{2,1,0:T(8,128)S(1)} fusion(f32[16,16,128]{2,1,0:T(8,128)S(1)} %fusion.33, f32[18,18,130]{2,1,0:T(8,128)S(1)} %select_maximum_fusion.8, f32[1,16,128]{2,1,0:T(8,128)S(1)} %collective-permute-done.32, f32[1,16,128]{2,1,0:T(8,128)S(1)} %collective-permute-done.31, f32[16,16,128]{2,1,0:T(8,128)S(1)} %copy-done, f32[]{:T(128)} %fusion.105, ...), kind=kLoop, calls=%fused_computation.100 | loop fusion | flops 1474560 | bytes 1065028 | tf_op jit(solution)/shard_map/add | solution.py:47
  376.3 2.6 collective-permute-done.33
  379.0 10.8 %fusion.23 = f32[16,16,128]{2,1,0:T(8,128)S(1)} fusion(f32[16,16,128]{2,1,0:T(8,128)S(1)} %fusion.28, f32[18,18,130]{2,1,0:T(8,128)S(1)} %select_maximum_fusion.6, f32[1,16,128]{2,1,0:T(8,128)S(1)} %collective-permute-done.34, f32[1,16,128]{2,1,0:T(8,128)S(1)} %collective-permute-done.33, f32[16,16,128]{2,1,0:T(8,128)S(1)} %copy-done, f32[]{:T(128)} %fusion.105, ...), kind=kLoop, calls=%fused_computation.89 | loop fusion | flops 1474560 | bytes 1065028 | tf_op jit(solution)/shard_map/add | solution.py:47
  394.2 2.6 collective-permute-done.35
  396.9 10.8 %fusion.18 = f32[16,16,128]{2,1,0:T(8,128)S(1)} fusion(f32[16,16,128]{2,1,0:T(8,128)S(1)} %fusion.23, f32[18,18,130]{2,1,0:T(8,128)S(1)} %select_maximum_fusion.4, f32[1,16,128]{2,1,0:T(8,128)S(1)} %collective-permute-done.36, f32[1,16,128]{2,1,0:T(8,128)S(1)} %collective-permute-done.35, f32[16,16,128]{2,1,0:T(8,128)S(1)} %copy-done, f32[]{:T(128)} %fusion.105, ...), kind=kLoop, calls=%fused_computation.78 | loop fusion | flops 1474560 | bytes 1065028 | tf_op jit(solution)/shard_map/add | solution.py:47
  412.1 2.6 collective-permute-done.37
  414.8 10.8 %fusion.13 = f32[16,16,128]{2,1,0:T(8,128)S(1)} fusion(f32[16,16,128]{2,1,0:T(8,128)S(1)} %fusion.18, f32[18,18,130]{2,1,0:T(8,128)S(1)} %select_maximum_fusion.2, f32[1,16,128]{2,1,0:T(8,128)S(1)} %collective-permute-done.38, f32[1,16,128]{2,1,0:T(8,128)S(1)} %collective-permute-done.37, f32[16,16,128]{2,1,0:T(8,128)S(1)} %copy-done, f32[]{:T(128)} %fusion.105, ...), kind=kLoop, calls=%fused_computation.67 | loop fusion | flops 1474560 | bytes 1065028 | tf_op jit(solution)/shard_map/add | solution.py:47
  427.6 2.6 collective-permute-start.39
  430.2 5.7 %reshape.51 = f32[4,4,4,4,32,4]{5,4,3,2,1,0:T(8,128)} reshape(f32[16,16,128]{2,1,0:T(8,128)S(1)} %collective-permute-done.20) | data formatting | bytes 262144 | tf_op jit(solution)/shard_map/reshape | solution.py:52
  435.8 2.6 reduce_sum.72
  438.6 10.8 %fusion.8 = f32[16,16,128]{2,1,0:T(8,128)S(1)} fusion(f32[16,16,128]{2,1,0:T(8,128)S(1)} %fusion.13, f32[18,18,130]{2,1,0:T(8,128)S(1)} %select_maximum_fusion, f32[1,16,128]{2,1,0:T(8,128)S(1)} %collective-permute-done.40, f32[1,16,128]{2,1,0:T(8,128)S(1)} %collective-permute-done.39, f32[16,16,128]{2,1,0:T(8,128)S(1)} %copy-done, f32[]{:T(128)} %fusion.105, ...), kind=kLoop, calls=%fused_computation.56 | loop fusion | flops 1474560 | bytes 1065028 | tf_op jit(solution)/shard_map/add | solution.py:47
  449.4 5.7 %reshape.50 = f32[4,4,4,4,32,4]{5,4,3,2,1,0:T(8,128)} reshape(f32[16,16,128]{2,1,0:T(8,128)S(1)} %fusion.8) | data formatting | bytes 262144 | tf_op jit(solution)/shard_map/reshape | solution.py:52
  455.1 2.6 reduce_sum.71
  458.2 18.8 %all_to_all.10 = f32[64,1,512]{2,1,0:T(1,128)S(1)} all-to-all(f32[64,1,512]{2,1,0:T(1,128)S(1)} %reshape.56), channel_id=1, replica_groups=mesh['tm'=64,'space'=8] {'tm'}, dimensions={0} | all-to-all | bytes 262144 | tf_op jit(solution)/shard_map/all_to_all | solution.py:79
  478.6 2.6 broadcast_in_dim.95
  481.2 4.9 reshape.53
  486.0 2.6 collective-permute-start.41
  488.6 13.7 %collective-permute-done.41 = f32[16,16,128]{2,1,0:T(8,128)S(1)} collective-permute-done((f32[16,16,128]{2,1,0:T(8,128)S(1)}, f32[16,16,128]{2,1,0:T(8,128)S(1)}, u32[]{:S(2)}, u32[]{:S(2)}) %collective-permute-start.41) | collective-permute-done | bytes 131104 | tf_op jit(solution)/shard_map/ppermute | solution.py:26
  (124 shorter events, 82.3 us)
Async XLA Ops:
  0.0 53.6 %copy-start = (f32[16,16,128]{2,1,0:T(8,128)S(1)}, f32[16,16,128]{2,1,0:T(8,128)}, u32[]{:S(2)}) copy-start(f32[16,16,128]{2,1,0:T(8,128)} %param.9) | copy-start | bytes 393220
  0.0 53.6 %copy-start.1 = (s32[16,16,128]{2,1,0:T(8,128)S(1)}, s32[16,16,128]{2,1,0:T(8,128)}, u32[]{:S(2)}) copy-start(s32[16,16,128]{2,1,0:T(8,128)} %param.8) | copy-start | bytes 393220
  0.8 13.9 %collective-permute-start.1 = (f32[1,16,128]{2,1,0:T(8,128)S(1)}, f32[1,16,128]{2,1,0:T(8,128)S(1)}, u32[]{:S(2)}, u32[]{:S(2)}) collective-permute-start(f32[1,16,128]{2,1,0:T(8,128)S(1)} %get-tuple-element.43), channel_id=1, source_target_pairs={{0,1},{1,2},{2,3},{3,4},{4,5},{5,6},{6,7},{8,9},{9,10},{10,11},{11... | collective-permute-start | bytes 24584 | tf_op jit(solution)/shard_map/ppermute | solution.py:15
  6.1 8.5 %collective-permute-start = (f32[1,16,128]{2,1,0:T(8,128)S(1)}, f32[1,16,128]{2,1,0:T(8,128)S(1)}, u32[]{:S(2)}, u32[]{:S(2)}) collective-permute-start(f32[1,16,128]{2,1,0:T(8,128)S(1)} %get-tuple-element.44), channel_id=1, source_target_pairs={{1,0},{2,1},{3,2},{4,3},{5,4},{6,5},{7,6},{9,8},{10,9},{11,10},{12... | collective-permute-start | bytes 24584 | tf_op jit(solution)/shard_map/ppermute | solution.py:18
  27.7 4.3 collective-permute-start.3
  29.6 5.0 collective-permute-start.2
  46.5 4.3 collective-permute-start.5
  48.5 5.0 collective-permute-start.4
  64.4 4.3 collective-permute-start.7
  66.4 5.4 %collective-permute-start.6 = (f32[1,16,128]{2,1,0:T(8,128)S(1)}, f32[1,16,128]{2,1,0:T(8,128)S(1)}, u32[]{:S(2)}, u32[]{:S(2)}) collective-permute-start(f32[1,16,128]{2,1,0:T(8,128)S(1)} %get-tuple-element.38), channel_id=1, source_target_pairs={{1,0},{2,1},{3,2},{4,3},{5,4},{6,5},{7,6},{9,8},{10,9},{11,10},{12... | collective-permute-start | bytes 24584 | tf_op jit(solution)/shard_map/ppermute | solution.py:18
  82.7 4.5 collective-permute-start.9
  84.7 92.0 %copy-start.2 = (f32[1,16,16,128]{3,2,1,0:T(8,128)S(1)}, f32[1,16,16,128]{3,2,1,0:T(8,128)}, u32[]{:S(2)}) copy-start(f32[1,16,16,128]{3,2,1,0:T(8,128)} %param.7) | copy-start | bytes 393220
  84.7 5.1 %collective-permute-start.8 = (f32[1,16,128]{2,1,0:T(8,128)S(1)}, f32[1,16,128]{2,1,0:T(8,128)S(1)}, u32[]{:S(2)}, u32[]{:S(2)}) collective-permute-start(f32[1,16,128]{2,1,0:T(8,128)S(1)} %get-tuple-element.36), channel_id=1, source_target_pairs={{1,0},{2,1},{3,2},{4,3},{5,4},{6,5},{7,6},{9,8},{10,9},{11,10},{12... | collective-permute-start | bytes 24584 | tf_op jit(solution)/shard_map/ppermute | solution.py:18
  100.8 4.3 collective-permute-start.11
  102.7 5.0 collective-permute-start.10
  118.6 4.3 collective-permute-start.13
  120.6 5.0 collective-permute-start.12
  136.5 4.3 collective-permute-start.15
  138.5 5.0 collective-permute-start.14
  154.4 4.3 collective-permute-start.17
  156.4 5.0 collective-permute-start.16
  172.3 12.6 %collective-permute-start.19 = (f32[1,16,128]{2,1,0:T(8,128)S(1)}, f32[1,16,128]{2,1,0:T(8,128)S(1)}, u32[]{:S(2)}, u32[]{:S(2)}) collective-permute-start(f32[1,16,128]{2,1,0:T(8,128)S(1)} %get-tuple-element.25), channel_id=1, source_target_pairs={{0,1},{1,2},{2,3},{3,4},{4,5},{5,6},{6,7},{8,9},{9,10},{10,11},{11... | collective-permute-start | bytes 24584 | tf_op jit(solution)/shard_map/ppermute | solution.py:15
  174.3 10.7 %collective-permute-start.18 = (f32[1,16,128]{2,1,0:T(8,128)S(1)}, f32[1,16,128]{2,1,0:T(8,128)S(1)}, u32[]{:S(2)}, u32[]{:S(2)}) collective-permute-start(f32[1,16,128]{2,1,0:T(8,128)S(1)} %get-tuple-element.26), channel_id=1, source_target_pairs={{1,0},{2,1},{3,2},{4,3},{5,4},{6,5},{7,6},{9,8},{10,9},{11,10},{12... | collective-permute-start | bytes 24584 | tf_op jit(solution)/shard_map/ppermute | solution.py:18
  195.9 8.3 %copy-start.3 = (f32[4,4,32]{2,1,0:T(4,128)S(1)}, f32[4,4,32]{2,1,0:T(4,128)}, u32[]{:S(2)}) copy-start(f32[4,4,32]{2,1,0:T(4,128)} %param.13) | copy-start | bytes 6148
  205.3 31.2 %all-to-all-start = ((f32[64,1,512]{2,1,0:T(1,128)}), f32[64,1,512]{2,1,0:T(1,128)S(1)}, u32[]{:S(2)}, u32[]{:S(2)}) async-start(f32[64,1,512]{2,1,0:T(1,128)} %reshape.54), calls=%async_computation | async-start | bytes 262144 | tf_op jit(solution)/shard_map/all_to_all | solution.py:79
  246.1 15.1 %collective-permute-start.20 = (f32[16,16,128]{2,1,0:T(8,128)S(1)}, f32[16,16,128]{2,1,0:T(8,128)S(1)}, u32[]{:S(2)}, u32[]{:S(2)}) collective-permute-start(f32[16,16,128]{2,1,0:T(8,128)S(1)} %add.550), channel_id=1, source_target_pairs={{504,0},{0,8},{8,16},{16,24},{24,32},{32,40},{40,48},{48,56},{56,6... | collective-permute-start | bytes 393224 | tf_op jit(solution)/shard_map/ppermute | solution.py:26
  261.2 6.3 %collective-permute-start.22 = (f32[1,16,128]{2,1,0:T(8,128)S(1)}, f32[1,16,128]{2,1,0:T(8,128)S(1)}, u32[]{:S(2)}, u32[]{:S(2)}) collective-permute-start(f32[1,16,128]{2,1,0:T(8,128)S(1)} %get-tuple-element.23), channel_id=1, source_target_pairs={{0,1},{1,2},{2,3},{3,4},{4,5},{5,6},{6,7},{8,9},{9,10},{10,11},{11... | collective-permute-start | bytes 24584 | tf_op jit(solution)/shard_map/ppermute | solution.py:15
  265.6 5.0 collective-permute-start.21
  281.6 4.3 collective-permute-start.24
  283.8 5.6 %collective-permute-start.23 = (f32[1,16,128]{2,1,0:T(8,128)S(1)}, f32[1,16,128]{2,1,0:T(8,128)S(1)}, u32[]{:S(2)}, u32[]{:S(2)}) collective-permute-start(f32[1,16,128]{2,1,0:T(8,128)S(1)} %get-tuple-element.22), channel_id=1, source_target_pairs={{1,0},{2,1},{3,2},{4,3},{5,4},{6,5},{7,6},{9,8},{10,9},{11,10},{12... | collective-permute-start | bytes 24584 | tf_op jit(solution)/shard_map/ppermute | solution.py:18
  300.4 4.3 collective-permute-start.26
  302.3 5.0 collective-permute-start.25
  318.3 4.3 collective-permute-start.28
  320.2 5.0 collective-permute-start.27
  336.1 4.3 collective-permute-start.30
  338.1 5.0 collective-permute-start.29
  354.0 4.3 collective-permute-start.32
  356.0 5.0 collective-permute-start.31
  371.9 4.3 collective-permute-start.34
  373.9 5.0 collective-permute-start.33
  389.8 4.3 collective-permute-start.36
  391.8 5.0 collective-permute-start.35
  407.7 4.3 collective-permute-start.38
  409.7 5.0 collective-permute-start.37
  425.6 12.9 %collective-permute-start.40 = (f32[1,16,128]{2,1,0:T(8,128)S(1)}, f32[1,16,128]{2,1,0:T(8,128)S(1)}, u32[]{:S(2)}, u32[]{:S(2)}) collective-permute-start(f32[1,16,128]{2,1,0:T(8,128)S(1)} %get-tuple-element.5), channel_id=1, source_target_pairs={{0,1},{1,2},{2,3},{3,4},{4,5},{5,6},{6,7},{8,9},{9,10},{10,11},{11... | collective-permute-start | bytes 24584 | tf_op jit(solution)/shard_map/ppermute | solution.py:15
  427.6 10.9 %collective-permute-start.39 = (f32[1,16,128]{2,1,0:T(8,128)S(1)}, f32[1,16,128]{2,1,0:T(8,128)S(1)}, u32[]{:S(2)}, u32[]{:S(2)}) collective-permute-start(f32[1,16,128]{2,1,0:T(8,128)S(1)} %get-tuple-element.6), channel_id=1, source_target_pairs={{1,0},{2,1},{3,2},{4,3},{5,4},{6,5},{7,6},{9,8},{10,9},{11,10},{12... | collective-permute-start | bytes 24584 | tf_op jit(solution)/shard_map/ppermute | solution.py:18
  486.0 16.3 %collective-permute-start.41 = (f32[16,16,128]{2,1,0:T(8,128)S(1)}, f32[16,16,128]{2,1,0:T(8,128)S(1)}, u32[]{:S(2)}, u32[]{:S(2)}) collective-permute-start(f32[16,16,128]{2,1,0:T(8,128)S(1)} %add.621), channel_id=1, source_target_pairs={{504,0},{0,8},{8,16},{16,24},{24,32},{32,40},{40,48},{48,56},{56,6... | collective-permute-start | bytes 393224 | tf_op jit(solution)/shard_map/ppermute | solution.py:26
